TPU v7x, 512 devices: a whole 4x8x8 slice. The times are simulated.
512 devices in a mesh: seq: 64 (over z, x, core), head: 8 (over y).
Axes of the slice: x: 4, y: 8, z: 8, core: 2. Of those that a mesh axis runs over, the one named last changes fastest.
Arguments:
- query_states: bfloat16 [16384, 4096], P(('seq', 'head')), may hold values from -8 to 8
- key_states: bfloat16 [16384, 4096], P(('seq', 'head')), may hold values from -8 to 8
- value_states: bfloat16 [16384, 4096], P(('seq', 'head')), may hold values from -8 to 8
- out_grad: bfloat16 [16384, 4096], P(('seq', 'head')), may hold values from -6 to 6
Outputs:
- attended: bfloat16 [16384, 4096], P('seq', 'head')
- query_grad: bfloat16 [16384, 4096], P('seq', 'head')
- key_grad: bfloat16 [16384, 4096], P('seq', 'head')
- value_grad: bfloat16 [16384, 4096], P('seq', 'head')
All inputs are finite; a program needn't handle non-finite values.
Results may differ from a plain program's by a relative error of at most 0.025.
Values may be sent and summed in bfloat16 or wider, within the bound.
A program may use at most 64 MiB of HBM per device.

v0:
```python
import jax
import jax.numpy as jnp
from jax import lax
from jax.sharding import PartitionSpec as P

HEAD_DIM = 128
BLOCK = 128


MASKED = -1e30


def broadcast(block, axis, owner):
    block = jnp.where(lax.axis_index(axis) == owner, block, jnp.zeros_like(block))
    return lax.psum(block, axis)


def with_halo(cells, sides, width):
    for axis, dim in sides:
        count = lax.axis_size(axis)
        ends = count - 1
        head = lax.slice_in_dim(cells, 0, width, axis=dim)
        tail = lax.slice_in_dim(cells, cells.shape[dim] - width, cells.shape[dim], axis=dim)
        cells = jnp.concatenate(
            [
                lax.ppermute(tail, axis, [(i, (i + 1) % count) for i in range(ends)]),
                cells,
                lax.ppermute(head, axis, [((i + 1) % count, i) for i in range(ends)]),
            ],
            axis=dim,
        )
    return cells


def shifted(value, axis, steps):
    count = lax.axis_size(axis)
    leading, last = (max(0, -steps), min(count, count - steps))
    return lax.ppermute(value, axis, [(source, source + steps) for source in range(leading, last)])


def local(query_states, key_states, value_states, out_grad):
    query_states, key_states, value_states, out_grad = (
        lax.all_to_all(query_states, "head", split_axis=1, concat_axis=0, tiled=True),
        lax.all_to_all(key_states, "head", split_axis=1, concat_axis=0, tiled=True),
        lax.all_to_all(value_states, "head", split_axis=1, concat_axis=0, tiled=True),
        lax.all_to_all(out_grad, "head", split_axis=1, concat_axis=0, tiled=True),
    )
    local_rows = query_states.shape[0]
    head_count = query_states.shape[1] // HEAD_DIM
    block_count = local_rows // BLOCK
    position = lax.axis_index("seq")
    total_blocks = block_count * lax.axis_size("seq")
    inverse_square_root = HEAD_DIM ** (-0.5)

    def as_blocks(array):
        return array.reshape(block_count, BLOCK, head_count, HEAD_DIM)

    def as_heads(array):
        return array.reshape(array.shape[0], head_count, HEAD_DIM)

    leading = jnp.stack(
        [query_states[:BLOCK], key_states[:BLOCK], value_states[:BLOCK], out_grad[:BLOCK]]
    )
    leading = broadcast(leading, "seq", 0)
    glob_query = as_heads(leading[0])
    glob_key = as_heads(leading[1])
    glob_value = as_heads(leading[2])
    glob_grad = as_heads(leading[3])
    extended = with_halo(jnp.stack([key_states, value_states]), (("seq", 1),), BLOCK)

    def windows(rows_ext, shared):
        spread = jnp.broadcast_to(shared[None], (block_count, BLOCK, head_count, HEAD_DIM))
        return jnp.concatenate(
            [
                spread,
                as_blocks(rows_ext[:local_rows]),
                as_blocks(rows_ext[BLOCK : BLOCK + local_rows]),
                as_blocks(rows_ext[2 * BLOCK :]),
            ],
            1,
        )

    window_key_rows = windows(extended[0], glob_key)
    window_value_rows = windows(extended[1], glob_value)
    block_ids = position * block_count + jnp.arange(block_count)
    allowed = jnp.stack(
        [block_ids >= 2, block_ids >= 1, block_ids >= 0, block_ids + 1 < total_blocks], 1
    )
    allowed = jnp.repeat(allowed, BLOCK, axis=1)[:, None, None, :]
    live_rows = (block_ids != 0)[:, None, None, None]
    query_blocks = as_blocks(query_states)
    grad_blocks = as_blocks(out_grad)
    logit_scores = (
        jnp.einsum(
            "cqhd,ckhd->chqk", query_blocks, window_key_rows, preferred_element_type=jnp.float32
        )
        * inverse_square_root
    )
    logit_scores = jnp.where(allowed, logit_scores, MASKED)
    row_top = jnp.max(logit_scores, -1, keepdims=True)
    log_total = row_top + jnp.log(jnp.sum(jnp.exp(logit_scores - row_top), -1, keepdims=True))
    weights = jnp.where(allowed & live_rows, jnp.exp(logit_scores - log_total), 0.0)
    probabilities = weights.astype(jnp.bfloat16)
    window_output = jnp.einsum(
        "chqk,ckhd->cqhd", probabilities, window_value_rows, preferred_element_type=jnp.float32
    ).astype(jnp.bfloat16)
    local_keys = as_heads(key_states)
    local_values = as_heads(value_states)
    glob_scores = (
        jnp.einsum("qhd,khd->hqk", glob_query, local_keys, preferred_element_type=jnp.float32)
        * inverse_square_root
    )
    local_top = jnp.max(glob_scores, -1)
    glob_top = lax.pmax(local_top, "seq")
    glob_total = lax.psum(jnp.sum(jnp.exp(glob_scores - glob_top[:, :, None]), -1), "seq")
    glob_log = glob_top + jnp.log(glob_total)
    glob_weights = jnp.exp(glob_scores - glob_log[:, :, None])
    glob_probs = glob_weights.astype(jnp.bfloat16)
    glob_part = jnp.einsum(
        "hqk,khd->qhd", glob_probs, local_values, preferred_element_type=jnp.float32
    )
    glob_out = lax.psum(glob_part, "seq").astype(jnp.bfloat16)
    glob_delta = jnp.sum(glob_grad.astype(jnp.float32) * glob_out.astype(jnp.float32), -1)
    glob_dprob = jnp.einsum(
        "qhd,khd->hqk", glob_grad, local_values, preferred_element_type=jnp.float32
    )
    glob_dscore = (glob_weights * (glob_dprob - glob_delta.T[:, :, None])).astype(jnp.bfloat16)
    glob_dquery_part = (
        jnp.einsum("hqk,khd->qhd", glob_dscore, local_keys, preferred_element_type=jnp.float32)
        * inverse_square_root
    )
    key_from_glob = (
        jnp.einsum("hqk,qhd->khd", glob_dscore, glob_query, preferred_element_type=jnp.float32)
        * inverse_square_root
    )
    value_from_glob = jnp.einsum(
        "hqk,qhd->khd", glob_probs, glob_grad, preferred_element_type=jnp.float32
    )
    band_delta = jnp.sum(
        grad_blocks.astype(jnp.float32) * window_output.astype(jnp.float32), -1
    ).transpose(0, 2, 1)
    probability_gradient = jnp.einsum(
        "cqhd,ckhd->chqk", grad_blocks, window_value_rows, preferred_element_type=jnp.float32
    )
    score_gradient = (weights * (probability_gradient - band_delta[:, :, :, None])).astype(
        jnp.bfloat16
    )
    window_query_gradient = (
        jnp.einsum(
            "chqk,ckhd->cqhd", score_gradient, window_key_rows, preferred_element_type=jnp.float32
        )
        * inverse_square_root
    )
    window_key_gradient = (
        jnp.einsum(
            "chqk,cqhd->ckhd", score_gradient, query_blocks, preferred_element_type=jnp.float32
        )
        * inverse_square_root
    )
    window_value_gradient = jnp.einsum(
        "chqk,cqhd->ckhd", probabilities, grad_blocks, preferred_element_type=jnp.float32
    )
    stacked = jnp.stack([window_key_gradient, window_value_gradient]).reshape(
        2, block_count, 4, BLOCK, head_count, HEAD_DIM
    )
    glob_piece = jnp.sum(stacked[:, :, 0], 1)
    before = stacked[:, :, 1]
    middle = stacked[:, :, 2]
    after = stacked[:, :, 3]
    empty_block = jnp.zeros((2, 1, BLOCK, head_count, HEAD_DIM), jnp.float32)
    inner = (
        middle
        + jnp.concatenate([before[:, 1:], empty_block], 1)
        + jnp.concatenate([empty_block, after[:, :-1]], 1)
    )
    from_right = shifted(before[:, 0].astype(jnp.bfloat16), "seq", -1).astype(jnp.float32)
    from_left = shifted(after[:, -1].astype(jnp.bfloat16), "seq", 1).astype(jnp.float32)
    inner = inner.at[:, 0].add(from_left)
    inner = inner.at[:, -1].add(from_right)
    glob_dquery, glob_dkey, glob_dvalue = lax.psum(
        (glob_dquery_part, glob_piece[0], glob_piece[1]), "seq"
    )
    local_grads = inner.reshape(2, local_rows, head_count, HEAD_DIM) + jnp.stack(
        [key_from_glob, value_from_glob]
    )
    is_first = ((jnp.arange(local_rows) < BLOCK) & (position == 0))[:, None, None]

    def padded(array):
        return jnp.concatenate(
            [array, jnp.zeros((local_rows - BLOCK,) + array.shape[1:], array.dtype)], 0
        )

    key_grad = local_grads[0] + jnp.where(is_first, padded(glob_dkey), 0.0)
    value_grad = local_grads[1] + jnp.where(is_first, padded(glob_dvalue), 0.0)
    query_grad = jnp.where(
        is_first,
        padded(glob_dquery),
        window_query_gradient.reshape(local_rows, head_count, HEAD_DIM),
    )
    attended = jnp.where(
        is_first, padded(glob_out), window_output.reshape(local_rows, head_count, HEAD_DIM)
    )
    return (
        attended.reshape(local_rows, -1),
        query_grad.reshape(local_rows, -1).astype(jnp.bfloat16),
        key_grad.reshape(local_rows, -1).astype(jnp.bfloat16),
        value_grad.reshape(local_rows, -1).astype(jnp.bfloat16),
    )


def solution(mesh):
    return jax.shard_map(
        local,
        mesh=mesh,
        in_specs=(
            P(("seq", "head"), None),
            P(("seq", "head"), None),
            P(("seq", "head"), None),
            P(("seq", "head"), None),
        ),
        out_specs=(P("seq", "head"), P("seq", "head"), P("seq", "head"), P("seq", "head")),
        check_vma=False,
    )
```

profile of v0, /device:TPU:26, one launch (start us, length us, event | category | flops | bytes accessed | tf_op | source)
XLA Modules:
  0.0 1251.6 jit_solution(274508605988238875)
XLA Ops:
  7.2 1.7 copy.193
  8.9 7.3 all-to-all-start
  16.2 1.7 copy.192
  17.9 6.6 all-to-all-done
  24.6 6.9 all-to-all-start.1
  32.2 6.2 all-to-all-done.1
  38.4 6.9 all-to-all-start.2
  46.0 6.5 all-to-all-done.2
  52.5 6.6 all-to-all-start.3
  59.3 7.0 all-to-all-done.3
  67.4 1.9 collective-permute-start
  69.4 3.6 collective-permute-start.1
  74.9 187.6 %all-reduce.12.cloned.1.call-done = bf16[4,128,512]{2,1,0:T(8,128)(2,1)} async-done(((bf16[4,128,512]{2,1,0:T(8,128)(2,1)}), bf16[4,128,512]{2,1,0:T(8,128)(2,1)}) %all-reduce.12.cloned.1.call-update) | async-done | bytes 524304 | tf_op jit(solution)/shard_map/psum | solution.py:15
  262.6 1.8 fusion.52
  267.8 1.8 fusion.36
  269.7 1.7 multiply_reduce_fusion
  271.5 1.7 fusion
  274.4 1.7 convolution_multiply_fusion
  276.2 1.9 copy.144
  278.1 2.9 copy.143
  281.0 2.4 fusion.20
  287.2 120.4 %pmax.7 = f32[4,128]{1,0:T(4,128)S(1)} all-reduce(f32[4,128]{1,0:T(4,128)S(1)} %get-tuple-element.71), channel_id=1, replica_groups=mesh['seq'=64,'head'=8] {'seq'}, use_global_device_ids=true, to_apply=%region_2.3 | all-reduce | flops 512 | bytes 4096 | tf_op jit(solution)/shard_map/pmax | solution.py:114
  407.9 124.1 %psum.43 = f32[4,128]{1,0:T(4,128)S(1)} all-reduce(f32[4,128]{1,0:T(4,128)S(1)} %exponential_reduce_fusion), channel_id=1, replica_groups=mesh['seq'=64,'head'=8] {'seq'}, use_global_device_ids=true, to_apply=%region_4.5 | all-reduce | flops 512 | bytes 4096 | tf_op jit(solution)/shard_map/psum | solution.py:115
  533.0 246.8 %all-reduce.15 = bf16[128,4,128]{0,2,1:T(8,128)(2,1)S(1)} all-reduce(f32[128,4,128]{0,2,1:T(8,128)} %convolution_bitcast_fusion.1), channel_id=1, replica_groups=mesh['seq'=64,'head'=8] {'seq'}, use_global_device_ids=true, to_apply=%region_5.6 | all-reduce | flops 65536 | bytes 393216 | tf_op jit(solution)/shard_map/psum | solution.py:122
  781.5 246.2 %all-reduce.16 = bf16[128,4,128]{0,2,1:T(8,128)(2,1)S(1)} all-reduce(f32[128,4,128]{0,2,1:T(8,128)S(1)} %fusion.10), channel_id=1, replica_groups=mesh['seq'=64,'head'=8] {'seq'}, use_global_device_ids=true, to_apply=%region_9.10 | all-reduce | flops 65536 | bytes 393216 | tf_op jit(solution)/shard_map/psum | solution.py:180
  1031.0 1.8 select_convert_fusion
  1032.8 1.9 copy.148
  1035.5 1.9 slice_bitcast_fusion.2
  1037.4 1.9 collective-permute-start.2
  1039.3 3.8 collective-permute-start.3
  1048.1 12.0 scatter-add.9
  1061.1 180.8 %all-reduce.14.cloned.1.call-done = (f32[128,4,128]{0,2,1:T(8,128)}, f32[128,4,128]{0,2,1:T(8,128)}) async-done(((f32[128,4,128]{0,2,1:T(8,128)}, f32[128,4,128]{0,2,1:T(8,128)}), (f32[128,4,128]{0,2,1:T(8,128)}, f32[128,4,128]{0,2,1:T(8,128)})) %all-reduce.14.cloned.1.call-update) | async-done | bytes 524304 | tf_op jit(solution)/shard_map/psum | solution.py:180
  (116 shorter events, 28.7 us)
Async XLA Ops:
  7.2 24.3 %copy-start.9 = (bf16[32,4096]{1,0:T(8,128)(2,1)S(1)}, bf16[32,4096]{1,0:T(8,128)(2,1)}, u32[]{:S(2)}) copy-start(bf16[32,4096]{1,0:T(8,128)(2,1)} %param.10) | copy-start | bytes 786436
  7.2 38.1 %copy-start.10 = (bf16[32,4096]{1,0:T(8,128)(2,1)S(1)}, bf16[32,4096]{1,0:T(8,128)(2,1)}, u32[]{:S(2)}) copy-start(bf16[32,4096]{1,0:T(8,128)(2,1)} %param.11) | copy-start | bytes 786436
  8.9 15.6 %all-to-all-start = ((bf16[32,8,512]{2,0,1:T(8,128)(2,1)}), bf16[32,8,512]{2,0,1:T(8,128)(2,1)S(1)}, u32[]{:S(2)}, u32[]{:S(2)}) async-start(bf16[32,8,512]{2,0,1:T(8,128)(2,1)} %bitcast.136), calls=%async_computation | async-start | bytes 524288 | tf_op jit(solution)/shard_map/all_to_all | solution.py:43
  24.6 13.9 %all-to-all-start.1 = ((bf16[32,8,512]{2,0,1:T(8,128)(2,1)}), bf16[32,8,512]{2,0,1:T(8,128)(2,1)S(1)}, u32[]{:S(2)}, u32[]{:S(2)}) async-start(bf16[32,8,512]{2,0,1:T(8,128)(2,1)} %bitcast.135), calls=%async_computation.1 | async-start | bytes 524288 | tf_op jit(solution)/shard_map/all_to_all | solution.py:44
  38.4 14.1 %all-to-all-start.2 = ((bf16[32,8,512]{2,0,1:T(8,128)(2,1)}), bf16[32,8,512]{2,0,1:T(8,128)(2,1)S(1)}, u32[]{:S(2)}, u32[]{:S(2)}) async-start(bf16[32,8,512]{2,0,1:T(8,128)(2,1)} %bitcast.134), calls=%async_computation.2 | async-start | bytes 524288 | tf_op jit(solution)/shard_map/all_to_all | solution.py:45
  52.5 13.8 %all-to-all-start.3 = ((bf16[32,8,512]{2,0,1:T(8,128)(2,1)}), bf16[32,8,512]{2,0,1:T(8,128)(2,1)S(1)}, u32[]{:S(2)}, u32[]{:S(2)}) async-start(bf16[32,8,512]{2,0,1:T(8,128)(2,1)} %bitcast.133), calls=%async_computation.3 | async-start | bytes 524288 | tf_op jit(solution)/shard_map/all_to_all | solution.py:46
  59.1 203.5 %all-reduce.12.cloned.1.call-start = ((), (), s32[]{:S(2)}) async-start(), calls=%async_computation.4 | async-start | bytes 1048576 | tf_op jit(solution)/shard_map/psum | solution.py:15
  67.3 1174.7 %all-reduce.14.cloned.1.call-start = ((), (), s32[]{:S(2)}) async-start(), calls=%async_computation.5 | async-start | bytes 1048576 | tf_op jit(solution)/shard_map/psum | solution.py:180
  67.4 197.1 %collective-permute-start = (bf16[2,128,512]{2,1,0:T(8,128)(2,1)S(1)}, bf16[2,128,512]{2,1,0:T(8,128)(2,1)}, u32[]{:S(2)}, u32[]{:S(2)}) collective-permute-start(bf16[2,128,512]{2,1,0:T(8,128)(2,1)S(1)} %get-tuple-element.63), channel_id=1, source_target_pairs={{0,8},{8,16},{16,24},{24,32},{32,40},{40,48},{48,56},{56,64},{64,7... | collective-permute-start | bytes 786440 | tf_op jit(solution)/shard_map/ppermute | solution.py:26
  69.4 195.2 %collective-permute-start.1 = (bf16[2,128,512]{2,1,0:T(8,128)(2,1)S(1)}, bf16[2,128,512]{2,1,0:T(8,128)(2,1)}, u32[]{:S(2)}, u32[]{:S(2)}) collective-permute-start(bf16[2,128,512]{2,1,0:T(8,128)(2,1)S(1)} %get-tuple-element.64), channel_id=1, source_target_pairs={{8,0},{16,8},{24,16},{32,24},{40,32},{48,40},{56,48},{64,56},{72,6... | collective-permute-start | bytes 786440 | tf_op jit(solution)/shard_map/ppermute | solution.py:28
  265.8 1.0 copy-start.11
  265.9 1.6 copy-start.13
  266.0 3.7 copy-start.15
  266.1 3.6 copy-start.16
  267.8 1.9 copy-start.12
  271.4 1.8 copy-start.14
  283.4 3.1 copy-start.8
  283.4 3.3 copy-start.7
  286.8 494.1 %copy-start.3 = (bf16[1,128,512]{1,2,0:T(8,128)(2,1)}, bf16[1,128,512]{1,2,0:T(8,128)(2,1)S(1)}, u32[]{:S(2)}) copy-start(bf16[1,128,512]{1,2,0:T(8,128)(2,1)S(1)} %copy.116) | copy-start | bytes 393220
  779.7 1.2 copy-start.5
  781.2 249.8 %copy-start.6 = (bf16[128,4,128]{0,2,1:T(8,128)(2,1)S(1)}, bf16[128,4,128]{0,2,1:T(8,128)(2,1)}, u32[]{:S(2)}) copy-start(bf16[128,4,128]{0,2,1:T(8,128)(2,1)} %copy-done.5) | copy-start | bytes 393220
  1031.0 12.1 copy-start.4
  1032.8 11.4 copy-start
  1037.4 8.1 collective-permute-start.2
  1039.3 8.2 collective-permute-start.3
  1047.5 13.5 %copy-start.1 = (f32[1,256,4,128]{1,3,2,0:T(8,128)S(1)}, f32[1,256,4,128]{1,3,2,0:T(8,128)}, u32[]{:S(2)}) copy-start(f32[1,256,4,128]{1,3,2,0:T(8,128)} %fusion.7) | copy-start | bytes 1572868
  1047.5 13.5 %copy-start.2 = (f32[1,256,4,128]{1,3,2,0:T(8,128)S(1)}, f32[1,256,4,128]{1,3,2,0:T(8,128)}, u32[]{:S(2)}) copy-start(f32[1,256,4,128]{1,3,2,0:T(8,128)} %convolution_bitcast_fusion) | copy-start | bytes 1572868
Sparse Core Ops, SparseCore 0:
  67.4 195.1 all-reduce.11
  1043.3 198.6 all-reduce.13
where the time goes:
time: 1250 us
  blocking collectives  737 us (59%)
  waiting for transfers between devices  395 us (32%)
  local copies, waits for them, and re-layouts  41.3 us (3%)
  starting transfers between devices  39 us (3%)
  between operations  14.6 us (1%)
  matrix products  13 us (1%)
    psum x1, blocking collectives, local(): glob_out = lax.psum(glob_part, 'seq').astype(jnp.bfloat16)  247 us
    psum x1, blocking collectives, local(): lax.psum((glob_dquery_part, glob_piece[0], glob_piece[1]), 'seq')  246 us
    psum x1, waiting for transfers between devices, broadcast(): return lax.psum(block, axis)  188 us
    psum x1, waiting for transfers between devices, local(): lax.psum((glob_dquery_part, glob_piece[0], glob_piece[1]), 'seq')  181 us
    psum x1, blocking collectives, local(): lax.psum(jnp.sum(jnp.exp(glob_scores - glob_top[:, :, None]), -1), 'seq')  124 us
    pmax x1, blocking collectives, local(): glob_top = lax.pmax(local_top, 'seq')  120 us
  transfers between devices with their start and end apart: 10, of which 6 were waited for; matrix products, arithmetic and copies ran while one was open for 2% of the time, Pallas kernels for 0%

commit v1 on v0

v1 whole, which is shorter than its diff:
```python
import jax
import jax.numpy as jnp
import numpy as np
from jax import lax
from jax.sharding import Mesh
from jax.sharding import PartitionSpec as P

HEAD_DIM = 128
BLOCK = 128


def seq_parts(mesh):
    column = mesh.devices[:, 0]
    count = column.shape[0]
    try:
        cores = len({d.core_on_chip for d in column})
        xs = len({d.coords[0] for d in column})
    except AttributeError:
        return (("s0", count),)
    parts = [("sz", count // (xs * cores)), ("sx", xs), ("sc", cores)]
    if parts[0][1] * xs * cores != count:
        return (("s0", count),)
    return tuple(p for p in parts if p[1] > 1) or (("s0", count),)


def make_local(parts):
    seq = tuple(name for name, _ in parts)
    seq_count = int(np.prod([size for _, size in parts]))

    def hpsum(value):
        for name in reversed(seq):
            value = lax.psum(value, name)
        return value

    def hgather(value):
        for name in reversed(seq):
            value = lax.all_gather(value, name, axis=0, tiled=True)
        return value

    def shifted(value, steps):
        leading, last = (max(0, -steps), min(seq_count, seq_count - steps))
        return lax.ppermute(value, seq, [(s, s + steps) for s in range(leading, last)])

    def local(query_states, key_states, value_states, out_grad):
        stacked = jnp.stack([query_states, key_states, value_states, out_grad])
        stacked = lax.all_to_all(stacked, "head", split_axis=2, concat_axis=1, tiled=True)
        local_rows = stacked.shape[1]
        head_count = stacked.shape[2] // HEAD_DIM
        block_count = local_rows // BLOCK
        position = lax.axis_index(seq)
        total_blocks = block_count * seq_count
        inverse_square_root = HEAD_DIM ** (-0.5)
        query_states, key_states, value_states, out_grad = (
            stacked[0], stacked[1], stacked[2], stacked[3]
        )

        def as_blocks(array):
            return array.reshape(block_count, BLOCK, head_count, HEAD_DIM)

        def as_heads(array):
            return array.reshape(array.shape[0], head_count, HEAD_DIM)

        leading = stacked[:, :BLOCK]
        leading = jnp.where(position == 0, leading, jnp.zeros_like(leading))
        leading = hpsum(leading)
        glob_query = as_heads(leading[0])
        glob_key = as_heads(leading[1])
        glob_value = as_heads(leading[2])
        glob_grad = as_heads(leading[3])

        kv = stacked[1:3]
        from_before = shifted(kv[:, local_rows - BLOCK :], 1)
        from_after = shifted(kv[:, :BLOCK], -1)
        extended = jnp.concatenate([from_before, kv, from_after], axis=1)

        def windows(rows_ext, shared):
            spread = jnp.broadcast_to(shared[None], (block_count, BLOCK, head_count, HEAD_DIM))
            return jnp.concatenate(
                [
                    spread,
                    as_blocks(rows_ext[:local_rows]),
                    as_blocks(rows_ext[BLOCK : BLOCK + local_rows]),
                    as_blocks(rows_ext[2 * BLOCK :]),
                ],
                1,
            )

        window_key_rows = windows(extended[0], glob_key)
        window_value_rows = windows(extended[1], glob_value)
        block_ids = position * block_count + jnp.arange(block_count)
        allowed = jnp.stack(
            [block_ids >= 2, block_ids >= 1, block_ids >= 0, block_ids + 1 < total_blocks], 1
        )
        allowed = jnp.repeat(allowed, BLOCK, axis=1)[:, None, None, :]
        live_rows = (block_ids != 0)[:, None, None, None]
        query_blocks = as_blocks(query_states)
        grad_blocks = as_blocks(out_grad)
        logit_scores = (
            jnp.einsum(
                "cqhd,ckhd->chqk", query_blocks, window_key_rows, preferred_element_type=jnp.float32
            )
            * inverse_square_root
        )
        logit_scores = jnp.where(allowed, logit_scores, -1e30)
        row_top = jnp.max(logit_scores, -1, keepdims=True)
        log_total = row_top + jnp.log(jnp.sum(jnp.exp(logit_scores - row_top), -1, keepdims=True))
        weights = jnp.where(allowed & live_rows, jnp.exp(logit_scores - log_total), 0.0)
        probabilities = weights.astype(jnp.bfloat16)
        window_output = jnp.einsum(
            "chqk,ckhd->cqhd", probabilities, window_value_rows, preferred_element_type=jnp.float32
        ).astype(jnp.bfloat16)

        local_keys = as_heads(key_states)
        local_values = as_heads(value_states)
        glob_scores = (
            jnp.einsum("qhd,khd->hqk", glob_query, local_keys, preferred_element_type=jnp.float32)
            * inverse_square_root
        )
        local_top = jnp.max(glob_scores, -1)
        local_exp = jnp.exp(glob_scores - local_top[:, :, None])
        local_sum = jnp.sum(local_exp, -1)
        local_out = jnp.einsum(
            "hqk,khd->hqd", local_exp, local_values.astype(jnp.float32),
            preferred_element_type=jnp.float32,
        )
        local_delta = jnp.sum(
            local_out * glob_grad.astype(jnp.float32).transpose(1, 0, 2), -1
        )
        stats = hgather(jnp.stack([local_top, local_sum, local_delta])[None])
        glob_top = jnp.max(stats[:, 0], 0)
        rescale = jnp.exp(stats[:, 0] - glob_top[None])
        glob_total = jnp.sum(rescale * stats[:, 1], 0)
        glob_log = glob_top + jnp.log(glob_total)
        glob_delta = jnp.sum(rescale * stats[:, 2], 0) / glob_total
        glob_weights = jnp.exp(glob_scores - glob_log[:, :, None])
        glob_probs = glob_weights.astype(jnp.bfloat16)
        glob_part = jnp.einsum(
            "hqk,khd->qhd", glob_probs, local_values, preferred_element_type=jnp.float32
        )
        glob_dprob = jnp.einsum(
            "qhd,khd->hqk", glob_grad, local_values, preferred_element_type=jnp.float32
        )
        glob_dscore = (glob_weights * (glob_dprob - glob_delta[:, :, None])).astype(jnp.bfloat16)
        glob_dquery_part = (
            jnp.einsum("hqk,khd->qhd", glob_dscore, local_keys, preferred_element_type=jnp.float32)
            * inverse_square_root
        )
        key_from_glob = (
            jnp.einsum("hqk,qhd->khd", glob_dscore, glob_query, preferred_element_type=jnp.float32)
            * inverse_square_root
        )
        value_from_glob = jnp.einsum(
            "hqk,qhd->khd", glob_probs, glob_grad, preferred_element_type=jnp.float32
        )
        band_delta = jnp.sum(
            grad_blocks.astype(jnp.float32) * window_output.astype(jnp.float32), -1
        ).transpose(0, 2, 1)
        probability_gradient = jnp.einsum(
            "cqhd,ckhd->chqk", grad_blocks, window_value_rows, preferred_element_type=jnp.float32
        )
        score_gradient = (weights * (probability_gradient - band_delta[:, :, :, None])).astype(
            jnp.bfloat16
        )
        window_query_gradient = (
            jnp.einsum(
                "chqk,ckhd->cqhd", score_gradient, window_key_rows, preferred_element_type=jnp.float32
            )
            * inverse_square_root
        )
        window_key_gradient = (
            jnp.einsum(
                "chqk,cqhd->ckhd", score_gradient, query_blocks, preferred_element_type=jnp.float32
            )
            * inverse_square_root
        )
        window_value_gradient = jnp.einsum(
            "chqk,cqhd->ckhd", probabilities, grad_blocks, preferred_element_type=jnp.float32
        )
        stacked_grads = jnp.stack([window_key_gradient, window_value_gradient]).reshape(
            2, block_count, 4, BLOCK, head_count, HEAD_DIM
        )
        glob_piece = jnp.sum(stacked_grads[:, :, 0], 1)
        before = stacked_grads[:, :, 1]
        middle = stacked_grads[:, :, 2]
        after = stacked_grads[:, :, 3]
        empty_block = jnp.zeros((2, 1, BLOCK, head_count, HEAD_DIM), jnp.float32)
        inner = (
            middle
            + jnp.concatenate([before[:, 1:], empty_block], 1)
            + jnp.concatenate([empty_block, after[:, :-1]], 1)
        )
        from_right = shifted(before[:, 0].astype(jnp.bfloat16), -1).astype(jnp.float32)
        from_left = shifted(after[:, -1].astype(jnp.bfloat16), 1).astype(jnp.float32)
        inner = inner.at[:, 0].add(from_left)
        inner = inner.at[:, -1].add(from_right)
        glob_out, glob_dquery, glob_dkey, glob_dvalue = hpsum(
            (glob_part, glob_dquery_part, glob_piece[0], glob_piece[1])
        )
        glob_out = glob_out.astype(jnp.bfloat16)
        local_grads = inner.reshape(2, local_rows, head_count, HEAD_DIM) + jnp.stack(
            [key_from_glob, value_from_glob]
        )
        is_first = ((jnp.arange(local_rows) < BLOCK) & (position == 0))[:, None, None]

        def padded(array):
            return jnp.concatenate(
                [array, jnp.zeros((local_rows - BLOCK,) + array.shape[1:], array.dtype)], 0
            )

        key_grad = local_grads[0] + jnp.where(is_first, padded(glob_dkey), 0.0)
        value_grad = local_grads[1] + jnp.where(is_first, padded(glob_dvalue), 0.0)
        query_grad = jnp.where(
            is_first,
            padded(glob_dquery),
            window_query_gradient.reshape(local_rows, head_count, HEAD_DIM),
        )
        attended = jnp.where(
            is_first, padded(glob_out), window_output.reshape(local_rows, head_count, HEAD_DIM)
        )
        return (
            attended.reshape(local_rows, -1),
            query_grad.reshape(local_rows, -1).astype(jnp.bfloat16),
            key_grad.reshape(local_rows, -1).astype(jnp.bfloat16),
            value_grad.reshape(local_rows, -1).astype(jnp.bfloat16),
        )

    return local, seq


def solution(mesh):
    parts = seq_parts(mesh)
    heads = mesh.shape["head"]
    names = tuple(name for name, _ in parts)
    sizes = tuple(size for _, size in parts)
    split_mesh = Mesh(mesh.devices.reshape(sizes + (heads,)), names + ("head",))
    local, seq = make_local(parts)
    spec_in = P(seq + ("head",), None)
    spec_out = P(seq, "head")
    return jax.shard_map(
        local,
        mesh=split_mesh,
        in_specs=(spec_in,) * 4,
        out_specs=(spec_out,) * 4,
        check_vma=False,
    )
```

time: 1250 us -> 491 us (0.39)
  the two profiles are of different devices: /device:TPU:26 before, /device:TPU:16 now
where the time goes in v1:
time: 491 us; the launch traced here: 490 us
  waiting for transfers between devices  293 us (60%)
  blocking collectives  78.6 us (16%)
  local copies, waits for them, and re-layouts  64.2 us (13%)
  starting transfers between devices  16.3 us (3%)
  between operations  14.7 us (3%)
  matrix products  12.6 us (3%)
  other arithmetic  10.3 us (2%)
    psum x6, waiting for transfers between devices, hpsum(): value = lax.psum(value, name)  271 us
    psum x1, blocking collectives, hpsum(): value = lax.psum(value, name)  39.6 us
    all_gather x3, blocking collectives, hgather(): value = lax.all_gather(value, name, axis=0, tiled=True)  39 us
    all_to_all x1, waiting for transfers between devices, local(): lax.all_to_all(stacked, 'head', split_axis=2, concat_axis=1, tiled=True)  22.4 us
    unnamed x45, local copies, waits for them, and re-layouts  20.4 us
    scatter-add x1, local copies, waits for them, and re-layouts, local(): inner = inner.at[:, -1].add(from_right)  12 us
    all_to_all x2, local copies, waits for them, and re-layouts, local(): lax.all_to_all(stacked, 'head', split_axis=2, concat_axis=1, tiled=True)  10.2 us
  transfers between devices with their start and end apart: 11, of which 7 were waited for; matrix products, arithmetic and copies ran while one was open for 8% of the time, Pallas kernels for 0%

profile of v1, /device:TPU:16, one launch (start us, length us, event | category | flops | bytes accessed | tf_op | source)
XLA Modules:
  0.0 490.1 jit_solution(11910787131558376043)
XLA Ops:
  7.2 1.3 pad_maximum_fusion
  8.5 4.6 copy.152
  13.1 7.8 %reshape.257 = bf16[8,2,32768]{2,1,0:T(2,128)(2,1)} reshape(bf16[4096,4,32]{2,1,0:T(4,128)(2,1)} %bitcast.155) | data formatting | bytes 2097152
  20.9 9.2 %all-to-all-start = ((bf16[8,2,32768]{2,1,0:T(2,128)(2,1)}), bf16[8,2,32768]{2,1,0:T(2,128)(2,1)S(1)}, u32[]{:S(2)}, u32[]{:S(2)}) async-start(bf16[8,2,32768]{2,1,0:T(2,128)(2,1)} %reshape.257), calls=%async_computation | async-start | bytes 2097152 | tf_op jit(solution)/shard_map/all_to_all | solution.py:46
  30.1 22.4 %all-to-all-done = bf16[8,2,32768]{2,1,0:T(2,128)(2,1)S(1)} async-done(((bf16[8,2,32768]{2,1,0:T(2,128)(2,1)}), bf16[8,2,32768]{2,1,0:T(2,128)(2,1)S(1)}, u32[]{:S(2)}, u32[]{:S(2)}) %all-to-all-start) | async-done | bytes 1048608 | tf_op jit(solution)/shard_map/all_to_all | solution.py:46
  52.5 4.5 reshape.258
  57.0 5.5 %copy.199 = bf16[4,32,8,512]{3,1,2,0:T(8,128)(2,1)S(1)} copy(bf16[4,32,8,512]{1,0,3,2:T(4,128)(2,1)} %bitcast.153) | data formatting | bytes 2097152 | tf_op jit(solution)/shard_map/all_to_all | solution.py:46
  63.5 38.7 %all-reduce.18.cloned.1.call-done = bf16[4,128,512]{2,1,0:T(8,128)(2,1)} async-done(((bf16[4,128,512]{2,1,0:T(8,128)(2,1)}), bf16[4,128,512]{2,1,0:T(8,128)(2,1)}) %all-reduce.18.cloned.1.call-update) | async-done | bytes 524304 | tf_op jit(solution)/shard_map/psum | solution.py:32
  102.4 4.7 copy.198
  107.3 2.9 collective-permute-start
  110.2 1.3 collective-permute-start.1
  111.5 48.1 %all-reduce.20.cloned.1.call-done = bf16[4,128,512]{2,1,0:T(8,128)(2,1)} async-done(((bf16[4,128,512]{2,1,0:T(8,128)(2,1)}), bf16[4,128,512]{2,1,0:T(8,128)(2,1)}) %all-reduce.20.cloned.1.call-update) | async-done | bytes 524304 | tf_op jit(solution)/shard_map/psum | solution.py:32
  164.9 77.7 %all-reduce.22.cloned.1.call-done = bf16[4,128,512]{2,1,0:T(8,128)(2,1)} async-done(((bf16[4,128,512]{2,1,0:T(8,128)(2,1)}), bf16[4,128,512]{2,1,0:T(8,128)(2,1)}) %all-reduce.22.cloned.1.call-update) | async-done | bytes 524304 | tf_op jit(solution)/shard_map/psum | solution.py:32
  245.7 1.8 all-gather
  247.5 12.2 %all_gather.10 = f32[8,3,4,128]{3,2,1,0:T(4,128)S(1)} all-gather(f32[2,3,4,128]{3,2,1,0:T(4,128)S(1)} %bitcast.176), channel_id=1, replica_groups=mesh['sz'=8,'sx'=4,'sc'=2,'head'=8] {'sx'}, dimensions={0}, use_global_device_ids=true | all-gather | bytes 61440 | tf_op jit(solution)/shard_map/all_gather | solution.py:37
  259.7 25.0 %all_gather.11 = f32[64,3,4,128]{3,2,1,0:T(4,128)S(1)} all-gather(f32[8,3,4,128]{3,2,1,0:T(4,128)S(1)} %all_gather.10), channel_id=1, replica_groups=mesh['sz'=8,'sx'=4,'sc'=2,'head'=8] {'sz'}, dimensions={0}, use_global_device_ids=true | all-gather | bytes 442368 | tf_op jit(solution)/shard_map/all_gather | solution.py:37
  289.8 1.3 multiply_reduce_fusion
  291.1 1.6 multiply_convert_fusion
  292.6 1.7 stack.63
  294.4 1.6 multiply_bitcast_fusion
  296.0 1.7 stack.62
  297.8 2.0 copy_dynamic-update-slice_fusion.1
  300.5 1.7 copy-done
  304.8 1.3 collective-permute-start.2
  306.8 1.3 collective-permute-start.3
  308.1 28.7 %all-reduce.28.cloned.1.call-done = (f32[128,4,128]{0,2,1:T(8,128)}, f32[128,4,128]{0,2,1:T(8,128)}, f32[128,4,128]{0,2,1:T(8,128)}, f32[128,4,128]{0,2,1:T(8,128)}) async-done(((f32[128,4,128]{0,2,1:T(8,128)}, f32[128,4,128]{0,2,1:T(8,128)}, f32[128,4,128]{0,2,1:T(8,128)}, f32[128,4,128]{0,2,1:T(8,128)}), (f32[128,4,128]{0,2,1:T(8,128)}, f32[128,4,128]{0,2,1:T(8,128)}, f32[128,4,128]{0,2,1:T(8,128)}, ...) | async-done | bytes 1048592 | tf_op jit(solution)/shard_map/psum | solution.py:32
  337.1 2.6 fusion.1
  339.7 1.4 fusion.9
  347.1 12.0 %scatter-add.9 = f32[2,2,128,4,128]{2,1,4,3,0:T(2,128)S(1)} dynamic-update-slice(f32[2,2,128,4,128]{2,1,4,3,0:T(2,128)S(1)} %copy.191, f32[2,1,128,4,128]{2,1,4,3,0:T(1,128)S(1)} %add.147, s32[]{:T(128)} %constant.93.clone.1, s32[]{:T(128)} %constant.98.clone.1, s32[]{:T(128)} %constant.93.clone.1, s32[]{:T(128)} %constant.93.clone.1, s32[]{:T(128)} %constant.93.clone.1) | dynamic-update-slice | bytes 1048580 | tf_op jit(solution)/shard_map/scatter-add | solution.py:195
  360.0 37.4 %all-reduce.26.cloned.1.call-done = (f32[128,4,128]{0,2,1:T(8,128)}, f32[128,4,128]{0,2,1:T(8,128)}, f32[128,4,128]{0,2,1:T(8,128)}, f32[128,4,128]{0,2,1:T(8,128)}) async-done(((f32[128,4,128]{0,2,1:T(8,128)}, f32[128,4,128]{0,2,1:T(8,128)}, f32[128,4,128]{0,2,1:T(8,128)}, f32[128,4,128]{0,2,1:T(8,128)}), (f32[128,4,128]{0,2,1:T(8,128)}, f32[128,4,128]{0,2,1:T(8,128)}, f32[128,4,128]{0,2,1:T(8,128)}, ...) | async-done | bytes 1048592 | tf_op jit(solution)/shard_map/psum | solution.py:32
  398.6 39.6 %all-reduce.29 = (bf16[128,4,128]{0,2,1:T(8,128)(2,1)S(1)}, bf16[128,4,128]{0,2,1:T(8,128)(2,1)S(1)}) all-reduce(f32[128,4,128]{0,2,1:T(8,128)S(1)} %copy-done.14, f32[128,4,128]{0,2,1:T(8,128)} %get-tuple-element.55), channel_id=1, replica_groups=mesh['sz'=8,'sx'=4,'sc'=2,'head'=8] {'sz'}, use_global_device_ids=true, to_apply=%region_10.11 | all-reduce | flops 131072 | bytes 786432 | tf_op jit(solution)/shard_map/psum | solution.py:32
  440.1 40.3 %all-reduce.24.cloned.1.call-done = (f32[128,4,128]{0,2,1:T(8,128)}, f32[128,4,128]{0,2,1:T(8,128)}) async-done(((f32[128,4,128]{0,2,1:T(8,128)}, f32[128,4,128]{0,2,1:T(8,128)}), (f32[128,4,128]{0,2,1:T(8,128)}, f32[128,4,128]{0,2,1:T(8,128)})) %all-reduce.24.cloned.1.call-update) | async-done | bytes 524304 | tf_op jit(solution)/shard_map/psum | solution.py:32
  (136 shorter events, 31.4 us)
Async XLA Ops:
  20.9 31.6 %all-to-all-start = ((bf16[8,2,32768]{2,1,0:T(2,128)(2,1)}), bf16[8,2,32768]{2,1,0:T(2,128)(2,1)S(1)}, u32[]{:S(2)}, u32[]{:S(2)}) async-start(bf16[8,2,32768]{2,1,0:T(2,128)(2,1)} %reshape.257), calls=%async_computation | async-start | bytes 2097152 | tf_op jit(solution)/shard_map/all_to_all | solution.py:46
  30.1 72.0 %all-reduce.18.cloned.1.call-start = ((), (), s32[]{:S(2)}) async-start(), calls=%async_computation.1 | async-start | bytes 1048576 | tf_op jit(solution)/shard_map/psum | solution.py:32
  63.4 96.2 %all-reduce.20.cloned.1.call-start = ((), (), s32[]{:S(2)}) async-start(), calls=%async_computation.2 | async-start | bytes 1048576 | tf_op jit(solution)/shard_map/psum | solution.py:32
  102.2 140.3 %all-reduce.22.cloned.1.call-start = ((), (), s32[]{:S(2)}) async-start(), calls=%async_computation.3 | async-start | bytes 1048576 | tf_op jit(solution)/shard_map/psum | solution.py:32
  107.3 54.5 %collective-permute-start = (bf16[2,128,512]{2,1,0:T(8,128)(2,1)S(1)}, bf16[2,128,512]{2,1,0:T(8,128)(2,1)}, u32[]{:S(2)}, u32[]{:S(2)}) collective-permute-start(bf16[2,128,512]{2,1,0:T(8,128)(2,1)S(1)} %get-tuple-element.83), channel_id=1, source_target_pairs={{0,8},{8,16},{16,24},{24,32},{32,40},{40,48},{48,56},{56,64},{64,7... | collective-permute-start | bytes 786440 | tf_op jit(solution)/shard_map/ppermute | solution.py:42
  110.2 51.6 %collective-permute-start.1 = (bf16[2,128,512]{2,1,0:T(8,128)(2,1)S(1)}, bf16[2,128,512]{2,1,0:T(8,128)(2,1)}, u32[]{:S(2)}, u32[]{:S(2)}) collective-permute-start(bf16[2,128,512]{2,1,0:T(8,128)(2,1)S(1)} %get-tuple-element.84), channel_id=1, source_target_pairs={{8,0},{16,8},{24,16},{32,24},{40,32},{48,40},{56,48},{64,56},{72,6... | collective-permute-start | bytes 786440 | tf_op jit(solution)/shard_map/ppermute | solution.py:42
  159.6 177.2 %all-reduce.28.cloned.1.call-start = ((), (), s32[]{:S(2)}) async-start(), calls=%async_computation.6 | async-start | bytes 2097152 | tf_op jit(solution)/shard_map/psum | solution.py:32
  161.3 126.0 %copy-start.9 = (bf16[2,128,4,128]{3,1,2,0:T(8,128)(2,1)}, bf16[2,128,4,128]{3,1,2,0:T(8,128)(2,1)S(1)}, u32[]{:S(2)}) copy-start(bf16[2,128,4,128]{3,1,2,0:T(8,128)(2,1)S(1)} %copy.175) | copy-start | bytes 786436
  163.1 124.1 %copy-start.10 = (bf16[2,128,4,128]{3,1,2,0:T(8,128)(2,1)}, bf16[2,128,4,128]{3,1,2,0:T(8,128)(2,1)S(1)}, u32[]{:S(2)}) copy-start(bf16[2,128,4,128]{3,1,2,0:T(8,128)(2,1)S(1)} %copy.174) | copy-start | bytes 786436
  164.9 122.4 %copy-start.11 = (bf16[2,128,4,128]{3,1,2,0:T(8,128)(2,1)}, bf16[2,128,4,128]{3,1,2,0:T(8,128)(2,1)S(1)}, u32[]{:S(2)}) copy-start(bf16[2,128,4,128]{3,1,2,0:T(8,128)(2,1)S(1)} %copy.176) | copy-start | bytes 786436
  244.7 41.3 %copy-start.3 = (bf16[1,128,512]{1,2,0:T(8,128)(2,1)}, bf16[1,128,512]{1,2,0:T(8,128)(2,1)S(1)}, u32[]{:S(2)}) copy-start(bf16[1,128,512]{1,2,0:T(8,128)(2,1)S(1)} %copy.156) | copy-start | bytes 393220
  287.3 0.7 copy-start.8
  288.6 0.9 copy-start.7
  288.6 1.0 copy-start.12
  288.6 1.1 copy-start.15
  288.6 1.2 copy-start.16
  297.8 2.2 copy-start.1
  300.2 2.0 copy-start
  303.0 94.3 %all-reduce.26.cloned.1.call-start = ((), (), s32[]{:S(2)}) async-start(), calls=%async_computation.5 | async-start | bytes 2097152 | tf_op jit(solution)/shard_map/psum | solution.py:32
  304.8 39.8 %collective-permute-start.2 = (bf16[2,128,4,128]{1,3,2,0:T(8,128)(2,1)}, bf16[2,128,4,128]{1,3,2,0:T(8,128)(2,1)S(1)}, u32[]{:S(2)}, u32[]{:S(2)}) collective-permute-start(bf16[2,128,4,128]{1,3,2,0:T(8,128)(2,1)} %fusion.17), channel_id=1, source_target_pairs={{0,8},{8,16},{16,24},{24,32},{32,40},{40,48},{48,56},{56,64},{64,7... | collective-permute-start | bytes 786440 | tf_op jit(solution)/shard_map/ppermute | solution.py:42
  306.8 38.7 %collective-permute-start.3 = (bf16[2,128,4,128]{1,3,2,0:T(8,128)(2,1)}, bf16[2,128,4,128]{1,3,2,0:T(8,128)(2,1)}, u32[]{:S(2)}, u32[]{:S(2)}) collective-permute-start(bf16[2,128,4,128]{1,3,2,0:T(8,128)(2,1)} %fusion.18), channel_id=1, source_target_pairs={{8,0},{16,8},{24,16},{32,24},{40,32},{48,40},{56,48},{64,56},{72,6... | collective-permute-start | bytes 786440 | tf_op jit(solution)/shard_map/ppermute | solution.py:42
  336.8 2.9 copy-start.2
  336.8 143.6 %all-reduce.24.cloned.1.call-start = ((), (), s32[]{:S(2)}) async-start(), calls=%async_computation.4 | async-start | bytes 1048576 | tf_op jit(solution)/shard_map/psum | solution.py:32
  339.7 2.5 copy-start.4
  341.1 1.4 copy-start.17
  341.1 2.4 copy-start.13
  397.3 1.3 copy-start.14
  397.3 40.9 %copy-start.5 = (bf16[256,4,128]{0,2,1:T(8,128)(2,1)S(1)}, bf16[256,4,128]{0,2,1:T(8,128)(2,1)}, u32[]{:S(2)}) copy-start(bf16[256,4,128]{0,2,1:T(8,128)(2,1)} %reshape.250) | copy-start | bytes 786436
  397.3 40.9 %copy-start.6 = (bf16[256,4,128]{0,2,1:T(8,128)(2,1)S(1)}, bf16[256,4,128]{0,2,1:T(8,128)(2,1)}, u32[]{:S(2)}) copy-start(bf16[256,4,128]{0,2,1:T(8,128)(2,1)} %reshape.248) | copy-start | bytes 786436
Sparse Core Ops, SparseCore 0:
  63.5 38.6 all-reduce.17
  104.6 54.9 all-reduce.19
  162.1 80.4 all-reduce.21
  303.2 33.6 all-reduce.27
  339.4 57.9 all-reduce.25
  399.6 80.8 all-reduce.23
